TPU v7x, 32 devices: a whole 2x2x4 slice. The times are simulated.
32 devices in a mesh: seq: 8 (over y, x, core), dp: 4 (over z).
Axes of the slice: x: 2, y: 2, z: 4, core: 2. Of those that a mesh axis runs over, the one named last changes fastest.
Arguments:
- queries: bfloat16 [4, 1024, 1536], P('dp', 'seq'), may hold values from -27 to 27
- keys: bfloat16 [4, 1024, 1536], P('dp', 'seq'), may hold values from -8 to 8
- values: bfloat16 [4, 1024, 1536], P('dp', 'seq'), may hold values from -6 to 6
- grad_out: bfloat16 [4, 1024, 1536], P('dp', 'seq'), may hold values from -6 to 6
- text_keys: bfloat16 [4, 64, 1536], P('dp', 'seq'), may hold values from -6 to 6
- text_values: bfloat16 [4, 64, 1536], P('dp', 'seq'), may hold values from -6 to 6
- null_keys: bfloat16 [64, 1536], replicated, may hold values from -6 to 6
- null_values: bfloat16 [64, 1536], replicated, may hold values from -6 to 6
- windows: int32 [64, 27], replicated, may hold values from -1 to 63, as said below
- tile_slot: int32 [64], replicated, may hold values from 0 to 63, as said below
- dropped: int32 [4], P('dp'), may hold values from 0 to 1, as said below
Outputs:
- grad_queries: bfloat16 [4, 1024, 1536], P('dp', 'seq')
- grad_keys: bfloat16 [4, 1024, 1536], P('dp', 'seq')
- grad_values: bfloat16 [4, 1024, 1536], P('dp', 'seq')
- grad_text_keys: bfloat16 [4, 64, 1536], P('dp', 'seq')
- grad_text_values: bfloat16 [4, 64, 1536], P('dp', 'seq')
- grad_null_keys: bfloat16 [64, 1536], replicated
- grad_null_values: bfloat16 [64, 1536], replicated
Inputs may be any that keep to these rules, and one draw needn't show every extreme that they name: `windows`: row t lists the key tiles of query tile t = 16 g + 4 r + c: every tile of the frame pairs g - 1, g, g + 1 that exist, in the tile rows d - 1, d, d + 1 for one d with |d - r| <= 1 and 1 <= d <= 2, and in the tile columns e - 1, e, e + 1 for one e with |e - c| <= 1 and 1 <= e <= 2; each once, in any order, the other entries -1. A permutation that keeps each frame pair's tiles among that pair's slots: tile_slot[t] // 16 == t // 16; slot s holds tile-order rows 16 s to 16 s + 15. `dropped`: at least one clip with 1 and one with 0.
All inputs are finite; a program needn't handle non-finite values.
Results may differ from a plain program's by a relative error of at most 0.012.
The roundings to bfloat16 on the way count: a program that leaves them out, or rounds other values in their place, can miss the bound.
Values may be sent and summed in bfloat16 or wider, within the bound.
A program may use at most 128 MiB of HBM per device.

v0:
```python
import functools

import jax
import jax.numpy as jnp
from jax import lax
from jax.experimental import pallas as pl
from jax.experimental.pallas import tpu as pltpu
from jax.sharding import PartitionSpec as P

HD = 128
FRAME_H = 8
FRAME_W = 16
TILE_T = 2
TILE_H = 2
TILE_W = 4


def partner(value, axis, stride):
    mask = 2**stride
    pairs = [(source, source ^ mask) for source in range(lax.axis_size(axis))]
    return lax.ppermute(value, axis, pairs)


def passed_along(x, axis, by):
    peers = lax.axis_size(axis)
    pairs = [(i, i + by) for i in range(peers) if 0 <= i + by < peers]
    return lax.ppermute(x, axis, pairs)


def tile_masked(scores, tile_allowed, tile_len, filler):
    head_count, query_rows, key_rows = scores.shape
    blocked = scores.reshape(
        head_count, query_rows // tile_len, tile_len, key_rows // tile_len, tile_len
    )
    blocked = jnp.where(tile_allowed[None, :, None, :, None], blocked, filler)
    return blocked.reshape(head_count, query_rows, key_rows)


def per_device(
    queries,
    keys,
    values,
    grad_out,
    text_keys,
    text_values,
    null_keys,
    null_values,
    windows,
    tile_slot,
    dropped,
):
    seq_count = lax.axis_size("seq")
    own_index = lax.axis_index("seq")
    local_rows = queries.shape[1]
    feature_count = queries.shape[2]
    head_size = HD
    head_count = feature_count // head_size
    score_scale = head_size ** (-0.5)
    tile_len = TILE_T * TILE_H * TILE_W
    tiles_local = local_rows // tile_len
    grid_w = FRAME_W // TILE_W
    grid_h = FRAME_H // TILE_H
    pair_len = grid_h * grid_w
    total_tiles = tiles_local * seq_count
    reach_devices = 3
    used_devices = 2 * reach_devices
    stacked = jnp.stack([queries[0], keys[0], values[0], grad_out[0]])
    halves = stacked.reshape(4, grid_h, TILE_H, grid_w, TILE_W, feature_count)
    halves = halves.transpose(0, 1, 3, 2, 4, 5).reshape(4, pair_len, TILE_H * TILE_W, feature_count)
    pair_index = own_index // 2
    parity = own_index % 2
    pair_slots = (
        lax.dynamic_slice_in_dim(tile_slot, pair_index * pair_len, pair_len) - pair_index * pair_len
    )
    slot_range = jnp.arange(pair_len, dtype=jnp.int32)
    local_tile = jnp.sum(
        jnp.where(pair_slots[None, :] == slot_range[:, None], slot_range[None, :], 0), axis=1
    )
    local_range = jnp.arange(tiles_local, dtype=jnp.int32)
    kept_halves = jnp.take(halves, local_tile[parity * tiles_local + local_range], axis=1)
    outgoing = jnp.take(halves, local_tile[(1 - parity) * tiles_local + local_range], axis=1)
    incoming = partner(outgoing, "seq", 0)
    first_half = jnp.where(parity == 0, kept_halves, incoming)
    second_half = jnp.where(parity == 0, incoming, kept_halves)
    tiled = jnp.concatenate([first_half, second_half], axis=2).reshape(4, local_rows, feature_count)
    tile_q = tiled[0]
    tile_k = tiled[1]
    tile_v = tiled[2]
    tile_go = tiled[3]
    slot_iota = jnp.arange(total_tiles, dtype=jnp.int32)
    slot_tile = jnp.sum(
        jnp.where(tile_slot[None, :] == slot_iota[:, None], slot_iota[None, :], 0), axis=1
    )
    query_ids = lax.dynamic_slice_in_dim(slot_tile, own_index * tiles_local, tiles_local)
    query_windows = jnp.take(windows, query_ids, axis=0)
    first_device = own_index - reach_devices + 1 - parity
    near_slots = first_device * tiles_local + jnp.arange(
        used_devices * tiles_local, dtype=jnp.int32
    )
    near_valid = (near_slots >= 0) & (near_slots < total_tiles)
    near_ids = jnp.where(
        near_valid, jnp.take(slot_tile, jnp.clip(near_slots, 0, total_tiles - 1)), -2
    )
    tile_allowed = jnp.any(query_windows[:, :, None] == near_ids[None, None, :], axis=1)
    pairs_kv = jnp.concatenate([tile_k, tile_v], axis=1)
    near_blocks = []
    for offset in range(-reach_devices, reach_devices + 1):
        if offset == 0:
            near_blocks.append(pairs_kv)
        else:
            near_blocks.append(passed_along(pairs_kv, "seq", -offset))
    near_all = jnp.concatenate(near_blocks, axis=0)
    near_kv = lax.dynamic_slice_in_dim(
        near_all, (1 - parity) * local_rows, used_devices * local_rows, 0
    )
    near_keys = near_kv[:, :feature_count].reshape(-1, head_count, head_size)
    near_values = near_kv[:, feature_count:].reshape(-1, head_count, head_size)
    prompt = lax.all_gather(
        jnp.concatenate([text_keys[0], text_values[0]], axis=1), "seq", axis=0, tiled=True
    )
    drop_flag = dropped[0]
    null_pair = jnp.concatenate([null_keys, null_values], axis=1)
    prompt_kv = jnp.where(drop_flag == 1, null_pair, prompt)
    prompt_keys = prompt_kv[:, :feature_count].reshape(-1, head_count, head_size)
    prompt_values = prompt_kv[:, feature_count:].reshape(-1, head_count, head_size)
    head_queries = tile_q.reshape(local_rows, head_count, head_size)
    head_grad_out = tile_go.reshape(local_rows, head_count, head_size)
    near_scores = (
        jnp.einsum("qhd,khd->hqk", head_queries, near_keys, preferred_element_type=jnp.float32)
        * score_scale
    )
    near_scores = tile_masked(near_scores, tile_allowed, tile_len, -jnp.inf)
    text_scores = (
        jnp.einsum("qhd,khd->hqk", head_queries, prompt_keys, preferred_element_type=jnp.float32)
        * score_scale
    )
    row_top = jnp.maximum(jnp.max(near_scores, axis=-1), jnp.max(text_scores, axis=-1))
    log_total = row_top + jnp.log(
        jnp.sum(jnp.exp(near_scores - row_top[..., None]), axis=-1)
        + jnp.sum(jnp.exp(text_scores - row_top[..., None]), axis=-1)
    )
    near_weights = jnp.exp(near_scores - log_total[..., None])
    text_weights = jnp.exp(text_scores - log_total[..., None])
    near_low = near_weights.astype(jnp.bfloat16)
    text_low = text_weights.astype(jnp.bfloat16)
    attended = jnp.einsum(
        "hqk,khd->qhd", near_low, near_values, preferred_element_type=jnp.float32
    ) + jnp.einsum("hqk,khd->qhd", text_low, prompt_values, preferred_element_type=jnp.float32)
    row_dot = jnp.transpose(jnp.sum(head_grad_out.astype(jnp.float32) * attended, axis=-1))
    near_grad_weights = jnp.einsum(
        "qhd,khd->hqk", head_grad_out, near_values, preferred_element_type=jnp.float32
    )
    text_grad_weights = jnp.einsum(
        "qhd,khd->hqk", head_grad_out, prompt_values, preferred_element_type=jnp.float32
    )
    near_grad_scores = (near_weights * (near_grad_weights - row_dot[..., None])).astype(
        jnp.bfloat16
    )
    text_grad_scores = (text_weights * (text_grad_weights - row_dot[..., None])).astype(
        jnp.bfloat16
    )
    grad_queries = (
        jnp.einsum("hqk,khd->qhd", near_grad_scores, near_keys, preferred_element_type=jnp.float32)
        + jnp.einsum(
            "hqk,khd->qhd", text_grad_scores, prompt_keys, preferred_element_type=jnp.float32
        )
    ) * score_scale
    grad_queries = grad_queries.reshape(local_rows, feature_count).astype(jnp.bfloat16)
    prompt_grad_k = (
        jnp.einsum(
            "hqk,qhd->khd", text_grad_scores, head_queries, preferred_element_type=jnp.float32
        )
        * score_scale
    )
    prompt_grad_v = jnp.einsum(
        "hqk,qhd->khd", text_low, head_grad_out, preferred_element_type=jnp.float32
    )
    prompt_partial = jnp.concatenate(
        [prompt_grad_k.reshape(-1, feature_count), prompt_grad_v.reshape(-1, feature_count)], axis=1
    )
    grad_total = jnp.zeros((local_rows, 2 * feature_count), jnp.float32)
    key_parts = (
        jnp.einsum(
            "hqk,qhd->khd", near_grad_scores, head_queries, preferred_element_type=jnp.float32
        )
        * score_scale
    ).astype(jnp.bfloat16)
    value_parts = jnp.einsum(
        "hqk,qhd->khd", near_low, head_grad_out, preferred_element_type=jnp.float32
    ).astype(jnp.bfloat16)
    contributions = jnp.concatenate(
        [key_parts.reshape(-1, feature_count), value_parts.reshape(-1, feature_count)], axis=1
    )
    empty_block = jnp.zeros((local_rows, 2 * feature_count), jnp.bfloat16)
    padded_parts = jnp.concatenate([empty_block, contributions, empty_block], axis=0)
    placed = lax.dynamic_slice_in_dim(
        padded_parts, parity * local_rows, (2 * reach_devices + 1) * local_rows, 0
    )
    for position, offset in enumerate(range(-reach_devices, reach_devices + 1)):
        outgoing_part = placed[position * local_rows : (position + 1) * local_rows]
        if offset == 0:
            grad_total = grad_total + outgoing_part.astype(jnp.float32)
        else:
            arrived = passed_along(outgoing_part, "seq", offset)
            grad_total = grad_total + arrived.astype(jnp.float32)
    grad_pairs = grad_total.astype(jnp.bfloat16)
    prompt_share = lax.psum_scatter(prompt_partial, "seq", scatter_dimension=0, tiled=True)
    drop_float = drop_flag.astype(jnp.float32)
    prompt_out = (prompt_share * (1.0 - drop_float)).astype(jnp.bfloat16)
    null_piece = lax.psum(prompt_share * drop_float, "dp").astype(jnp.bfloat16)
    null_out = lax.all_gather(null_piece, "seq", axis=0, tiled=True)
    return (
        grad_queries[None],
        grad_pairs[:, :feature_count][None],
        grad_pairs[:, feature_count:][None],
        prompt_out[:, :feature_count][None],
        prompt_out[:, feature_count:][None],
        null_out[:, :feature_count],
        null_out[:, feature_count:],
    )


HEADS_PER_PAIR = 3
SLOTS = 2
NT = (((1,), (1,)), ((), ()))
TN = (((0,), (0,)), ((), ()))
BLOCKED = -1e30


def dot(a, b, dims=(((1,), (0,)), ((), ()))):
    return lax.dot_general(a, b, dims, preferred_element_type=jnp.float32)


def head_kernel(
    seq_count,
    dp_count,
    q_ref,
    k_ref,
    v_ref,
    go_ref,
    tk_ref,
    tv_ref,
    nk_ref,
    nv_ref,
    windows_ref,
    slot_ref,
    drop_ref,
    dq_ref,
    dk_ref,
    dv_ref,
    dtk_ref,
    dtv_ref,
    dnk_ref,
    dnv_ref,
    inbuf,
    textbuf,
    nullbuf,
    outbuf,
    tgrad,
    zall,
    nsum,
    bias,
    perm,
    acc_k,
    acc_v,
    in_send,
    in_recv,
    text_send,
    text_recv,
    null_sem,
    out_send,
    out_recv,
    tg_send,
    tg_recv,
    z_send,
    z_recv,
    n_send,
    n_recv,
    own_null,
    r_send,
    sib_recv,
    windows_vmem,
    slot_vmem,
    drop_smem,
    small_sem,
):
    me = lax.axis_index("seq")
    clip = lax.axis_index("dp")
    chip = me // 2
    parity = me % 2
    chips = seq_count // 2
    rows = q_ref.shape[1]
    text_rows = tk_ref.shape[1]
    prompt_rows = seq_count * text_rows
    pair_rows = 2 * rows
    score_scale = HD**-0.5
    tokens = (q_ref, k_ref, v_ref, go_ref)
    texts = (tk_ref, tv_ref)
    own_slots = SLOTS - parity

    def columns(head):
        return pl.ds(pl.multiple_of(head * HD, HD), HD)

    def head_of(device, slot):
        first = HEADS_PER_PAIR * (device // 2)
        if isinstance(slot, int):
            return first + (device % 2 if slot == 0 else 2)
        return first + (1 - slot) * (device % 2) + 2 * slot

    own_row = pl.ds(pl.multiple_of(me * rows, rows), rows)

    def inward(slot, place, dest, act):
        cols = columns(head_of(dest, slot))
        for t in range(4):
            act(
                pltpu.make_async_remote_copy(
                    src_ref=tokens[t].at[0, :, cols],
                    dst_ref=inbuf.at[slot, t, own_row, :],
                    send_sem=in_send.at[slot, place, t],
                    recv_sem=in_recv.at[slot, t],
                    device_id={"seq": dest},
                    device_id_type=pl.DeviceIdType.MESH,
                )
            )
        for t in range(2):
            act(
                pltpu.make_async_remote_copy(
                    src_ref=texts[t].at[0, :, cols],
                    dst_ref=textbuf.at[slot, t, me],
                    send_sem=text_send.at[slot, place, t],
                    recv_sem=text_recv.at[slot, t],
                    device_id={"seq": dest},
                    device_id_type=pl.DeviceIdType.MESH,
                )
            )

    def inward_own(slot):
        cols = columns(head_of(me, slot))
        for t in range(4):
            pltpu.make_async_copy(
                tokens[t].at[0, :, cols], inbuf.at[slot, t, own_row, :], in_recv.at[slot, t]
            ).start()
        for t in range(2):
            pltpu.make_async_copy(
                texts[t].at[0, :, cols], textbuf.at[slot, t, me], text_recv.at[slot, t]
            ).start()
        for t, ref in enumerate((nk_ref, nv_ref)):
            pltpu.make_async_copy(ref.at[:, cols], nullbuf.at[slot, t], null_sem.at[slot, t]).start()

    def all_inward(act):
        for off in range(1, seq_count):
            inward(0, off, (me + off) % seq_count, act)
        for off in range(1, chips):
            inward(1, off, 2 * ((chip + off) % chips), act)

        @pl.when(parity == 1)
        def _():
            inward(1, 0, 2 * chip, act)

    outs = (dq_ref, dk_ref, dv_ref)
    text_outs = (dtk_ref, dtv_ref)
    null_outs = (dnk_ref, dnv_ref)

    def outward(slot, off, act, which=(0, 1, 2)):
        dest = (me + off) % seq_count
        cols = columns(head_of(me, slot))
        dest_row = pl.ds(pl.multiple_of(dest * rows, rows), rows)
        for t in which:
            act(
                pltpu.make_async_remote_copy(
                    src_ref=outbuf.at[slot, t, dest_row, :],
                    dst_ref=outs[t].at[0, :, cols],
                    send_sem=out_send.at[slot, off, t],
                    recv_sem=out_recv.at[t],
                    device_id={"seq": dest},
                    device_id_type=pl.DeviceIdType.MESH,
                )
            )
        for t in range(2) if 0 in which else ():
            act(
                pltpu.make_async_remote_copy(
                    src_ref=tgrad.at[slot, t, dest],
                    dst_ref=text_outs[t].at[0, :, cols],
                    send_sem=tg_send.at[slot, off, t],
                    recv_sem=tg_recv.at[t],
                    device_id={"seq": dest},
                    device_id_type=pl.DeviceIdType.MESH,
                )
            )

    def outward_own(slot):
        cols = columns(head_of(me, slot))
        for t in range(3):
            pltpu.make_async_copy(
                outbuf.at[slot, t, own_row, :], outs[t].at[0, :, cols], out_recv.at[t]
            ).start()
        for t in range(2):
            pltpu.make_async_copy(
                tgrad.at[slot, t, me], text_outs[t].at[0, :, cols], tg_recv.at[t]
            ).start()

    def across_clips(slot, off):
        return pltpu.make_async_remote_copy(
            src_ref=zall.at[slot, clip],
            dst_ref=zall.at[slot, clip],
            send_sem=z_send.at[slot, off],
            recv_sem=z_recv.at[slot],
            device_id={"dp": (clip + off) % dp_count},
            device_id_type=pl.DeviceIdType.MESH,
        )

    sibling = me + 1 - 2 * parity

    def null_copy(src, t, cols, send_sem, recv_sem, dest):
        return pltpu.make_async_remote_copy(
            src_ref=src,
            dst_ref=null_outs[t].at[:, cols],
            send_sem=send_sem,
            recv_sem=recv_sem,
            device_id={"seq": dest},
            device_id_type=pl.DeviceIdType.MESH,
        )

    def null_outward(slot, act):
        cols = columns(head_of(me, slot))
        for t in range(2):
            for off in range(1, chips):
                dest = 2 * ((chip + off) % chips) + parity
                sems = n_send.at[slot, off, t], n_recv.at[slot, t]
                act(null_copy(nsum.at[slot, t], t, cols, *sems, dest))
            sems = n_send.at[slot, 0, t], sib_recv.at[slot, 0, t]
            act(null_copy(nsum.at[slot, t], t, cols, *sems, sibling))

    def null_relay(slot, act):
        for t in range(2):
            for off in range(1, chips):
                source = 2 * ((chip + off) % chips) + parity
                cols = columns(head_of(source, slot))
                sems = r_send.at[slot, off, t], sib_recv.at[slot, off, t]
                act(null_copy(null_outs[t].at[:, cols], t, cols, *sems, sibling))

    def start(copy):
        copy.start()

    def sent(copy):
        copy.wait_send()

    def landed(ref, sem):
        pltpu.make_async_copy(ref, ref, sem).wait()

    small = [
        pltpu.make_async_copy(windows_ref, windows_vmem, small_sem.at[0]),
        pltpu.make_async_copy(slot_ref, slot_vmem, small_sem.at[1]),
        pltpu.make_async_copy(drop_ref, drop_smem, small_sem.at[2]),
    ]
    barrier = pltpu.get_barrier_semaphore()
    for off in range(1, seq_count):
        pl.semaphore_signal(
            barrier,
            inc=1,
            device_id={"seq": (me + off) % seq_count},
            device_id_type=pl.DeviceIdType.MESH,
        )
    for off in range(1, dp_count):
        pl.semaphore_signal(
            barrier,
            inc=1,
            device_id={"dp": (clip + off) % dp_count},
            device_id_type=pl.DeviceIdType.MESH,
        )
    for copy in small:
        copy.start()
    pl.semaphore_wait(barrier, seq_count - 1 + dp_count - 1)
    all_inward(start)
    inward_own(0)

    @pl.when(parity == 0)
    def _():
        inward_own(1)

    for copy in small:
        copy.wait()

    total_rows = seq_count * rows
    tile_count = windows_ref.shape[1]
    grid_w = FRAME_W // TILE_W
    pair_tiles = tile_count // chips
    tile_len = TILE_T * TILE_H * TILE_W

    def tile_of(token):
        inside = token % rows
        return (
            pair_tiles * (token // pair_rows)
            + grid_w * (inside // FRAME_W // TILE_H)
            + inside % FRAME_W // TILE_W
        )

    token = lax.broadcasted_iota(jnp.int32, (total_rows, tile_count), 0)
    tile = lax.broadcasted_iota(jnp.int32, (total_rows, tile_count), 1)
    member = jnp.where(tile_of(token) == tile, 1.0, 0.0).astype(jnp.bfloat16)
    listed = jnp.zeros((tile_count, tile_count), jnp.float32)
    key_tile = lax.broadcasted_iota(jnp.int32, (tile_count, tile_count), 0)
    for entry in range(windows_ref.shape[0]):
        listed = jnp.where(windows_vmem[entry : entry + 1, :] == key_tile, 1.0, listed)
    by_key = dot(member, listed.astype(jnp.bfloat16)).astype(jnp.bfloat16)
    spans = []
    for pair in range(chips):
        low, high = max(pair - 1, 0) * pair_rows, min(pair + 2, chips) * pair_rows
        spans.append((low, high))
        own = slice(pair * pair_rows, (pair + 1) * pair_rows)
        allowed = dot(by_key[low:high], member[own], NT)
        bias[pair, : high - low, :] = (1.0 - allowed) * BLOCKED
        slots = jnp.broadcast_to(slot_vmem[...].astype(jnp.float32), (8, tile_count))
        slot_row = dot(slots.astype(jnp.bfloat16), member[own], NT)[0:1]
        n = lax.broadcasted_iota(jnp.int32, (1, pair_rows), 1)
        inside = n % rows
        place = (
            (n // rows) * (TILE_H * TILE_W)
            + (inside // FRAME_W % TILE_H) * TILE_W
            + inside % TILE_W
        )
        target = (slot_row.astype(jnp.int32) - pair * pair_tiles) * tile_len + place
        row = lax.broadcasted_iota(jnp.int32, (pair_rows, pair_rows), 0)
        perm[pair] = jnp.where(row == target, 1.0, 0.0).astype(jnp.bfloat16)

    is_dropped = drop_smem[0] == 1

    def null_sum(slot):
        landed(zall.at[slot, pl.ds(0, dp_count - 1)], z_recv.at[slot])
        total = zall[slot, 0]
        for peer in range(1, dp_count):
            total = total + zall[slot, peer]
        for t in range(2):
            nsum[slot, t] = total[t * prompt_rows : (t + 1) * prompt_rows].astype(jnp.bfloat16)
        cols = columns(head_of(me, slot))
        null_outward(slot, start)
        for t in range(2):
            pltpu.make_async_copy(
                nsum.at[slot, t], null_outs[t].at[:, cols], own_null.at[slot, t]
            ).start()

    def one_head(slot, carry):
        for t in range(4):
            landed(inbuf.at[slot, t], in_recv.at[slot, t])
        for t in range(2):
            landed(textbuf.at[slot, t], text_recv.at[slot, t])
            landed(nullbuf.at[slot, t], null_sem.at[slot, t])
        prompt = []
        for t in range(2):
            text = textbuf[slot, t].astype(jnp.float32).reshape(prompt_rows, HD)
            null = nullbuf[slot, t].astype(jnp.float32)
            prompt.append(jnp.where(is_dropped, null, text).astype(jnp.bfloat16))
        prompt_k, prompt_v = prompt
        prompt_dk = jnp.zeros((prompt_rows, HD), jnp.float32)
        prompt_dv = jnp.zeros((prompt_rows, HD), jnp.float32)
        acc_k[...] = jnp.zeros_like(acc_k)
        acc_v[...] = jnp.zeros_like(acc_v)
        for pair in range(chips):
            low, high = spans[pair]
            own = slice(pair * pair_rows, (pair + 1) * pair_rows)
            q = inbuf[slot, 0, own, :]
            go = inbuf[slot, 3, own, :]
            near_k = inbuf[slot, 1, low:high, :]
            near_v = inbuf[slot, 2, low:high, :]
            near = dot(near_k, q, NT) * score_scale + bias[pair, : high - low, :]
            text = dot(prompt_k, q, NT) * score_scale
            top = jnp.maximum(
                jnp.max(near, axis=0, keepdims=True), jnp.max(text, axis=0, keepdims=True)
            )
            near = jnp.exp(near - top)
            text = jnp.exp(text - top)
            share = 1.0 / (
                jnp.sum(near, axis=0, keepdims=True) + jnp.sum(text, axis=0, keepdims=True)
            )
            near = near * share
            text = text * share
            near_low = near.astype(jnp.bfloat16)
            text_low = text.astype(jnp.bfloat16)
            near_g = dot(near_v, go, NT)
            text_g = dot(prompt_v, go, NT)
            row_dot = jnp.sum(
                near_low.astype(jnp.float32) * near_g, axis=0, keepdims=True
            ) + jnp.sum(text_low.astype(jnp.float32) * text_g, axis=0, keepdims=True)
            near_ds = (near * (near_g - row_dot)).astype(jnp.bfloat16)
            text_ds = (text * (text_g - row_dot)).astype(jnp.bfloat16)
            dq = (dot(near_ds, near_k, TN) + dot(text_ds, prompt_k, TN)) * score_scale
            outbuf[slot, 0, own, :] = dot(perm[pair], dq.astype(jnp.bfloat16)).astype(jnp.bfloat16)
            acc_k[low:high, :] += dot(near_ds, q)
            acc_v[low:high, :] += dot(near_low, go)
            prompt_dk += dot(text_ds, q)
            prompt_dv += dot(text_low, go)
        prompt_dk = prompt_dk * score_scale
        drop_scale = jnp.where(is_dropped, 1.0, 0.0)
        keep_scale = 1.0 - drop_scale
        for t, grad in enumerate((prompt_dk, prompt_dv)):
            kept = (grad * keep_scale).reshape(seq_count, text_rows, HD)
            tgrad[slot, t] = kept.astype(jnp.bfloat16)
            zall[slot, clip, t * prompt_rows : (t + 1) * prompt_rows, :] = grad * drop_scale
        for off in range(1, dp_count):
            across_clips(slot, off).start()
        for off in range(1, seq_count):
            outward(slot, off, start, (0,))
        for pair in range(chips):
            own = slice(pair * pair_rows, (pair + 1) * pair_rows)
            dk = (acc_k[own, :] * score_scale).astype(jnp.bfloat16)
            outbuf[slot, 1, own, :] = dot(perm[pair], dk).astype(jnp.bfloat16)
            dv = acc_v[own, :].astype(jnp.bfloat16)
            outbuf[slot, 2, own, :] = dot(perm[pair], dv).astype(jnp.bfloat16)
        null_sum(slot)
        for off in range(1, seq_count):
            outward(slot, off, start, (1, 2))
        outward_own(slot)
        return carry

    lax.fori_loop(0, own_slots, one_head, 0)

    def pass_on(slot, carry):
        for t in range(2):
            landed(null_outs[t].at[:, 0 : (chips - 1) * HD], n_recv.at[slot, t])
        null_relay(slot, start)
        return carry

    lax.fori_loop(0, own_slots, pass_on, 0)

    all_inward(sent)

    def drain(slot, carry):
        for off in range(1, dp_count):
            across_clips(slot, off).wait_send()
        for off in range(1, seq_count):
            outward(slot, off, sent)
        null_outward(slot, sent)
        null_relay(slot, sent)
        for t in range(2):
            landed(nsum.at[slot, t], own_null.at[slot, t])
        return carry

    def from_sibling(slot, carry):
        for t in range(2):
            for place in range(chips):
                landed(null_outs[t].at[:, 0:HD], sib_recv.at[slot, place, t])
        return carry

    lax.fori_loop(0, own_slots, drain, 0)
    for t in range(3):
        landed(outs[t], out_recv.at[t])
    for t in range(2):
        landed(text_outs[t], tg_recv.at[t])
    lax.fori_loop(0, 1 + parity, from_sibling, 0)


def hand_over(*refs):
    count = (len(refs) - 2) // 3
    sources, results, held = refs[:count], refs[count : 2 * count], refs[2 * count : 3 * count]
    into, out_of = refs[3 * count :]
    loads = [pltpu.make_async_copy(sources[i], held[i], into.at[i]) for i in range(count)]
    stores = [pltpu.make_async_copy(held[i], results[i], out_of.at[i]) for i in range(count)]
    for load in loads:
        load.start()
    for load, store in zip(loads, stores):
        load.wait()
        store.start()
    for store in stores:
        store.wait()


def by_heads(
    dp_count,
    queries,
    keys,
    values,
    grad_out,
    text_keys,
    text_values,
    null_keys,
    null_values,
    windows,
    tile_slot,
    dropped,
):
    seq_count = lax.axis_size("seq")
    rows = queries.shape[1]
    total_rows = seq_count * rows
    pair_rows = 2 * rows
    text_rows = text_keys.shape[1]
    prompt_rows = text_rows * seq_count
    chips = seq_count // 2
    bf16, f32 = jnp.bfloat16, jnp.float32
    dma = pltpu.SemaphoreType.DMA
    hbm = pl.BlockSpec(memory_space=pl.ANY)
    like = [queries, keys, values, text_keys, text_values, null_keys, null_values]
    gathered = pl.pallas_call(
        functools.partial(head_kernel, seq_count, dp_count),
        out_shape=tuple(jax.ShapeDtypeStruct(x.shape, x.dtype) for x in like),
        in_specs=[hbm] * 11,
        out_specs=tuple([hbm] * 7),
        scratch_shapes=[
            pltpu.VMEM((SLOTS, 4, total_rows, HD), bf16),
            pltpu.VMEM((SLOTS, 2, seq_count, text_rows, HD), bf16),
            pltpu.VMEM((SLOTS, 2, prompt_rows, HD), bf16),
            pltpu.VMEM((SLOTS, 3, total_rows, HD), bf16),
            pltpu.VMEM((SLOTS, 2, seq_count, text_rows, HD), bf16),
            pltpu.VMEM((SLOTS, dp_count, 2 * prompt_rows, HD), f32),
            pltpu.VMEM((SLOTS, 2, prompt_rows, HD), bf16),
            pltpu.VMEM((chips, 3 * pair_rows, pair_rows), f32),
            pltpu.VMEM((chips, pair_rows, pair_rows), bf16),
            pltpu.VMEM((total_rows, HD), f32),
            pltpu.VMEM((total_rows, HD), f32),
            dma((SLOTS, seq_count, 4)),
            dma((SLOTS, 4)),
            dma((SLOTS, seq_count, 2)),
            dma((SLOTS, 2)),
            dma((SLOTS, 2)),
            dma((SLOTS, seq_count, 3)),
            dma((3,)),
            dma((SLOTS, seq_count, 2)),
            dma((2,)),
            dma((SLOTS, dp_count)),
            dma((SLOTS,)),
            dma((SLOTS, chips, 2)),
            dma((SLOTS, 2)),
            dma((SLOTS, 2)),
            dma((SLOTS, chips, 2)),
            dma((SLOTS, chips, 2)),
            pltpu.VMEM(windows.shape[::-1], jnp.int32),
            pltpu.VMEM((1, tile_slot.shape[0]), jnp.int32),
            pltpu.SMEM(dropped.shape, jnp.int32),
            dma((3,)),
        ],
        compiler_params=pltpu.CompilerParams(
            collective_id=0, has_side_effects=True, vmem_limit_bytes=56 * 2**20
        ),
    )(
        queries,
        keys,
        values,
        grad_out,
        text_keys,
        text_values,
        null_keys,
        null_values,
        windows.T,
        tile_slot.reshape(1, -1),
        dropped,
    )
    return pl.pallas_call(
        hand_over,
        out_shape=tuple(jax.ShapeDtypeStruct(x.shape, x.dtype) for x in like),
        in_specs=[hbm] * 7,
        out_specs=tuple([hbm] * 7),
        scratch_shapes=[pltpu.VMEM(x.shape, x.dtype) for x in like] + [dma((7,)), dma((7,))],
    )(*gathered)


def device_program(mesh):
    seq_count, dp_count = mesh.shape["seq"], mesh.shape["dp"]

    def program(*arrays):
        head_count = arrays[0].shape[2] // HD
        if seq_count % 2 == 0 and 2 * head_count == HEADS_PER_PAIR * seq_count:
            return by_heads(dp_count, *arrays)
        return per_device(*arrays)

    return program


def solution(mesh):
    in_specs = (
        P("dp", "seq", None),
        P("dp", "seq", None),
        P("dp", "seq", None),
        P("dp", "seq", None),
        P("dp", "seq", None),
        P("dp", "seq", None),
        P(),
        P(),
        P(),
        P(),
        P("dp"),
    )
    out_specs = (
        P("dp", "seq", None),
        P("dp", "seq", None),
        P("dp", "seq", None),
        P("dp", "seq", None),
        P("dp", "seq", None),
        P(),
        P(),
    )
    return jax.shard_map(
        device_program(mesh), mesh=mesh, in_specs=in_specs, out_specs=out_specs, check_vma=False
    )
```

profile of v0, /device:TPU:1, one launch (start us, length us, event | category | flops | bytes accessed | tf_op | source)
XLA Modules:
  0.0 48.0 jit_solution(1495532545603771809)
XLA Ops:
  1.3 44.5 %shard_map.162 = (bf16[1,128,1536]{2,1,0:T(8,128)(2,1)}, bf16[1,128,1536]{2,1,0:T(8,128)(2,1)}, bf16[1,128,1536]{2,1,0:T(8,128)(2,1)}, bf16[1,8,1536]{2,1,0:T(8,...) custom-call(bf16[1,128,1536]{2,1,0:T(8,128)(2,1)} %q_ref.1, ...), custom_call_target="tpu_custom_call" | custom-call | tf_op jit(solution)/shard_map/pallas_call | solution.py:692
  45.7 2.3 %shard_map.163 = (bf16[1,128,1536]{2,1,0:T(8,128)(2,1)}, bf16[1,128,1536]{2,1,0:T(8,128)(2,1)}, bf16[1,128,1536]{2,1,0:T(8,128)(2,1)}, bf16[1,8,1536]{2,1,0:T(8,...) custom-call(bf16[1,128,1536]{2,1,0:T(8,128)(2,1)} %get-tuple-element.14.refs_0_, ...), custom_call_target="tpu_custom_call" | custom-call | tf_op jit(solution)/shard_map/pallas_call | solution.py:746
where the time goes:
time: 48.2 us; the launch traced here: 48 us
  Pallas kernels  46.7 us (97%)
  between operations  1.29 us (3%)
    pallas_call x1, Pallas kernels, by_heads(): pl.pallas_call(functools.partial(head_kernel, seq_count, dp_count), out_s...  44.5 us
    pallas_call x1, Pallas kernels, by_heads(): pl.pallas_call(hand_over, out_shape=tuple((jax.ShapeDtypeStruct(x.shape,...  2.27 us

commit v1 on v0

--- a/solution.py
+++ b/solution.py
@@ -598,6 +598,11 @@
             zall[slot, clip, t * prompt_rows : (t + 1) * prompt_rows, :] = grad * drop_scale
         for off in range(1, dp_count):
             across_clips(slot, off).start()
+
+        @pl.when(slot == 1)
+        def _():
+            null_sum(0)
+
         for off in range(1, seq_count):
             outward(slot, off, start, (0,))
         for pair in range(chips):
@@ -606,13 +611,13 @@
             outbuf[slot, 1, own, :] = dot(perm[pair], dk).astype(jnp.bfloat16)
             dv = acc_v[own, :].astype(jnp.bfloat16)
             outbuf[slot, 2, own, :] = dot(perm[pair], dv).astype(jnp.bfloat16)
-        null_sum(slot)
         for off in range(1, seq_count):
             outward(slot, off, start, (1, 2))
         outward_own(slot)
         return carry
 
     lax.fori_loop(0, own_slots, one_head, 0)
+    null_sum(own_slots - 1)
 
     def pass_on(slot, carry):
         for t in range(2):
@@ -650,15 +655,10 @@
 
 
 def hand_over(*refs):
-    count = (len(refs) - 2) // 3
-    sources, results, held = refs[:count], refs[count : 2 * count], refs[2 * count : 3 * count]
-    into, out_of = refs[3 * count :]
-    loads = [pltpu.make_async_copy(sources[i], held[i], into.at[i]) for i in range(count)]
-    stores = [pltpu.make_async_copy(held[i], results[i], out_of.at[i]) for i in range(count)]
-    for load in loads:
-        load.start()
-    for load, store in zip(loads, stores):
-        load.wait()
+    count = (len(refs) - 1) // 2
+    sources, results, out_of = refs[:count], refs[count : 2 * count], refs[2 * count]
+    stores = [pltpu.make_async_copy(sources[i], results[i], out_of.at[i]) for i in range(count)]
+    for store in stores:
         store.start()
     for store in stores:
         store.wait()
@@ -728,19 +728,24 @@
             dma((3,)),
         ],
         compiler_params=pltpu.CompilerParams(
-            collective_id=0, has_side_effects=True, vmem_limit_bytes=56 * 2**20
+            collective_id=0, has_side_effects=True, vmem_limit_bytes=24 * 2**20
         ),
     )(
-        queries,
-        keys,
-        values,
-        grad_out,
-        text_keys,
-        text_values,
-        null_keys,
-        null_values,
-        windows.T,
-        tile_slot.reshape(1, -1),
+        *(
+            pltpu.with_memory_space_constraint(x, pltpu.HBM)
+            for x in (
+                queries,
+                keys,
+                values,
+                grad_out,
+                text_keys,
+                text_values,
+                null_keys,
+                null_values,
+                windows.T,
+                tile_slot.reshape(1, -1),
+            )
+        ),
         dropped,
     )
     return pl.pallas_call(
@@ -748,7 +753,8 @@
         out_shape=tuple(jax.ShapeDtypeStruct(x.shape, x.dtype) for x in like),
         in_specs=[hbm] * 7,
         out_specs=tuple([hbm] * 7),
-        scratch_shapes=[pltpu.VMEM(x.shape, x.dtype) for x in like] + [dma((7,)), dma((7,))],
+        scratch_shapes=[dma((7,))],
+        compiler_params=pltpu.CompilerParams(vmem_limit_bytes=2 * 2**20),
     )(*gathered)
 
 

time: 48.2 us -> 46.8 us (0.971)
  Pallas kernels: 46.7 us -> 45.2 us
    pallas_call x1, Pallas kernels: 2.27 us -> 1.21 us  [by_heads(): pl.pallas_call(hand_over, out_shape=tuple((jax.ShapeDtypeStruct(x.shape,...]
where the time goes in v1:
time: 46.8 us; the launch traced here: 46.5 us
  Pallas kernels  45.2 us (97%)
  between operations  1.29 us (3%)
    pallas_call x1, Pallas kernels, by_heads(): pl.pallas_call(functools.partial(head_kernel, seq_count, dp_count), out_s...  44 us
    pallas_call x1, Pallas kernels, by_heads(): pl.pallas_call(hand_over, out_shape=tuple((jax.ShapeDtypeStruct(x.shape,...  1.21 us

profile of v1, /device:TPU:1, one launch (start us, length us, event | category | flops | bytes accessed | tf_op | source)
XLA Modules:
  0.0 46.5 jit_solution(13461790313529287319)
XLA Ops:
  1.3 44.0 %shard_map.162 = (bf16[1,128,1536]{2,1,0:T(8,128)(2,1)S(1)}, bf16[1,128,1536]{2,1,0:T(8,128)(2,1)S(1)}, bf16[1,128,1536]{2,1,0:T(8,128)(2,1)S(1)}, bf16[1,8,1536...) custom-call(bf16[1,128,1536]{2,1,0:T(8,128)(2,1)} %q_ref.1, ...), custom_call_target="tpu_custom_call" | custom-call | tf_op jit(solution)/shard_map/pallas_call | solution.py:692
  45.3 1.2 %shard_map.163 = (bf16[1,128,1536]{2,1,0:T(8,128)(2,1)}, bf16[1,128,1536]{2,1,0:T(8,128)(2,1)}, bf16[1,128,1536]{2,1,0:T(8,128)(2,1)}, bf16[1,8,1536]{2,1,0:T(8,...) custom-call(bf16[1,128,1536]{2,1,0:T(8,128)(2,1)S(1)} %get-tuple-element.14.refs_0_, ...), custom_call_target="tpu_custom_call" | custom-call | tf_op jit(solution)/shard_map/pallas_call | solution.py:751

commit v2 on v1

--- a/solution.py
+++ b/solution.py
@@ -527,9 +527,9 @@
 
     def null_sum(slot):
         landed(zall.at[slot, pl.ds(0, dp_count - 1)], z_recv.at[slot])
-        total = zall[slot, 0]
+        total = zall[slot, 0].astype(jnp.float32)
         for peer in range(1, dp_count):
-            total = total + zall[slot, peer]
+            total = total + zall[slot, peer].astype(jnp.float32)
         for t in range(2):
             nsum[slot, t] = total[t * prompt_rows : (t + 1) * prompt_rows].astype(jnp.bfloat16)
         cols = columns(head_of(me, slot))
@@ -595,7 +595,9 @@
         for t, grad in enumerate((prompt_dk, prompt_dv)):
             kept = (grad * keep_scale).reshape(seq_count, text_rows, HD)
             tgrad[slot, t] = kept.astype(jnp.bfloat16)
-            zall[slot, clip, t * prompt_rows : (t + 1) * prompt_rows, :] = grad * drop_scale
+            zall[slot, clip, t * prompt_rows : (t + 1) * prompt_rows, :] = (
+                grad * drop_scale
+            ).astype(jnp.bfloat16)
         for off in range(1, dp_count):
             across_clips(slot, off).start()
 
@@ -611,13 +613,22 @@
             outbuf[slot, 1, own, :] = dot(perm[pair], dk).astype(jnp.bfloat16)
             dv = acc_v[own, :].astype(jnp.bfloat16)
             outbuf[slot, 2, own, :] = dot(perm[pair], dv).astype(jnp.bfloat16)
+
+        @pl.when(slot == 1)
+        def _():
+            null_sum(slot)
+
         for off in range(1, seq_count):
             outward(slot, off, start, (1, 2))
         outward_own(slot)
         return carry
 
     lax.fori_loop(0, own_slots, one_head, 0)
-    null_sum(own_slots - 1)
+
+    @pl.when(parity == 1)
+    def _():
+        null_sum(0)
+
 
     def pass_on(slot, carry):
         for t in range(2):
@@ -700,7 +711,7 @@
             pltpu.VMEM((SLOTS, 2, prompt_rows, HD), bf16),
             pltpu.VMEM((SLOTS, 3, total_rows, HD), bf16),
             pltpu.VMEM((SLOTS, 2, seq_count, text_rows, HD), bf16),
-            pltpu.VMEM((SLOTS, dp_count, 2 * prompt_rows, HD), f32),
+            pltpu.VMEM((SLOTS, dp_count, 2 * prompt_rows, HD), bf16),
             pltpu.VMEM((SLOTS, 2, prompt_rows, HD), bf16),
             pltpu.VMEM((chips, 3 * pair_rows, pair_rows), f32),
             pltpu.VMEM((chips, pair_rows, pair_rows), bf16),

time: 46.8 us -> 44.5 us (0.951)
  Pallas kernels: 45.2 us -> 43 us
    pallas_call x1, Pallas kernels: 44 us -> 41.8 us  [by_heads(): pl.pallas_call(functools.partial(head_kernel, seq_count, dp_count), out_s...]
where the time goes in v2:
time: 44.5 us; the launch traced here: 44.3 us
  Pallas kernels  43 us (97%)
  between operations  1.29 us (3%)
    pallas_call x1, Pallas kernels, by_heads(): pl.pallas_call(functools.partial(head_kernel, seq_count, dp_count), out_s...  41.8 us
    pallas_call x1, Pallas kernels, by_heads(): pl.pallas_call(hand_over, out_shape=tuple((jax.ShapeDtypeStruct(x.shape,...  1.21 us

profile of v2, /device:TPU:1, one launch (start us, length us, event | category | flops | bytes accessed | tf_op | source)
XLA Modules:
  0.0 44.3 jit_solution(17177906558286547236)
XLA Ops:
  1.3 41.8 %shard_map.162 = (bf16[1,128,1536]{2,1,0:T(8,128)(2,1)S(1)}, bf16[1,128,1536]{2,1,0:T(8,128)(2,1)S(1)}, bf16[1,128,1536]{2,1,0:T(8,128)(2,1)S(1)}, bf16[1,8,1536...) custom-call(bf16[1,128,1536]{2,1,0:T(8,128)(2,1)} %q_ref.1, ...), custom_call_target="tpu_custom_call" | custom-call | tf_op jit(solution)/shard_map/pallas_call | solution.py:703
  43.1 1.2 %shard_map.163 = (bf16[1,128,1536]{2,1,0:T(8,128)(2,1)}, bf16[1,128,1536]{2,1,0:T(8,128)(2,1)}, bf16[1,128,1536]{2,1,0:T(8,128)(2,1)}, bf16[1,8,1536]{2,1,0:T(8,...) custom-call(bf16[1,128,1536]{2,1,0:T(8,128)(2,1)S(1)} %get-tuple-element.14.refs_0_, ...), custom_call_target="tpu_custom_call" | custom-call | tf_op jit(solution)/shard_map/pallas_call | solution.py:762
